TPU v7x, 512 devices: a whole 4x4x16 slice. The times are simulated.
512 devices in a mesh: pix: 64 (over z, y), train: 8 (over x, core).
Axes of the slice: x: 4, y: 4, z: 16, core: 2. Of those that a mesh axis runs over, the one named last changes fastest.
Arguments:
- raw_frames: bfloat16 [24, 352, 16384], P('train', None, 'pix'), may hold values from 60 to 160
- gain_section: int32 [24, 352, 16384], P('train', None, 'pix'), may hold values from 0 to 2
- dark_offset: bfloat16 [3, 352, 16384], P(None, None, 'pix'), may hold values from 0 to 40
- rel_gain: float32 [3, 16384], P(None, 'pix'), may hold values from 0.5 to 8
- cycle_label: int32 [16384, 1], P('pix'), may hold values from 0 to 191; in each aligned block of 256 rows (0 to 255, 256 to 511, ...) at most 2 rows name the same one
- cycle_slot: int32 [192], replicated, may hold values from 0 to 191, each once
Outputs:
- two_time: float32 [192, 352, 352], P('pix', 'train')
Inputs may be any that keep to these rules, and one draw needn't show every extreme that they name: `cycle_label`: among the pixels of one index of pix no cycle holds more than 2 pixels; every cycle holds some pixel. `cycle_slot`: A permutation of the cycles.
All inputs are finite; a program needn't handle non-finite values.
Results may differ from a plain program's by a relative error of at most 0.0003.
Values sent between devices are 32-bit elements; how exact they have to be, the bound alone decides.
A program may use at most 64 MiB of HBM per device.

v0:
```python
import jax
import jax.numpy as jnp
from jax import lax
from jax.sharding import PartitionSpec as P

CYCLE_DEV = 3


def on_device(raw_frames, gain_section, dark_offset, rel_gain, cycle_label, cycle_slot):
    trains, pulses, pixels = raw_frames.shape
    owners = lax.axis_size("pix")
    cycle_count = CYCLE_DEV * owners
    slot_depth = 2 * pixels // cycle_count
    section_zero = gain_section == 0
    section_one = gain_section == 1
    offset = jnp.where(
        section_zero, dark_offset[0], jnp.where(section_one, dark_offset[1], dark_offset[2])
    ).astype(jnp.float32)
    factor = jnp.where(section_zero, rel_gain[0], jnp.where(section_one, rel_gain[1], rel_gain[2]))
    intensity = (raw_frames.astype(jnp.float32) - offset) * factor
    pixel_rows = jnp.transpose(intensity, (2, 0, 1)).reshape(pixels, trains * pulses)
    labels = cycle_label[:, 0]
    member = labels[:, None] == jnp.arange(cycle_count, dtype=jnp.int32)[None, :]
    slot_of = jnp.sum(jnp.where(member, cycle_slot[None, :], 0), axis=1)
    running = jnp.cumsum(member.astype(jnp.int32), axis=0)
    within_cycle = jnp.sum(jnp.where(member, running, 0), axis=1) - 1
    cycle_counts = jnp.sum(member.astype(jnp.int32), axis=0)
    slot_member = cycle_slot[:, None] == jnp.arange(cycle_count, dtype=jnp.int32)[None, :]
    slot_counts = jnp.sum(jnp.where(slot_member, cycle_counts[:, None], 0), axis=0)
    position = slot_of * slot_depth + within_cycle
    buffer = (
        jnp.zeros((cycle_count * slot_depth, trains * pulses), jnp.float32)
        .at[position]
        .set(pixel_rows)
    )
    buffer = buffer.reshape(owners, CYCLE_DEV, slot_depth, trains * pulses)
    cycle_tally = slot_counts.astype(jnp.float32).reshape(owners, CYCLE_DEV, 1)
    slot_data = lax.all_to_all(buffer, "pix", split_axis=0, concat_axis=2, tiled=True)
    numbers = lax.all_to_all(cycle_tally, "pix", split_axis=0, concat_axis=2, tiled=True)
    item_count = slot_data.shape[1]
    blocks = slot_data.reshape(item_count, slot_data.shape[2], trains, pulses)
    gram_sum = jnp.einsum("kstf,kstg->kfg", blocks, blocks, precision=lax.Precision.HIGHEST)
    frame_means = jnp.sum(blocks, axis=(1, 2))
    gram_sum, frame_means, number = (
        gram_sum,
        frame_means,
        jnp.sum(numbers.reshape(item_count, numbers.shape[2]), axis=1),
    )
    groups = lax.axis_size("train")
    all_trains = trains * groups
    row_band = pulses // groups
    row_start = lax.axis_index("train") * row_band
    gram_whole, means_whole = lax.psum((gram_sum, frame_means), "train")
    gram_rows = lax.dynamic_slice_in_dim(gram_whole, row_start, row_band, 1)
    means_rows = lax.dynamic_slice_in_dim(means_whole, row_start, row_band, 1)
    cycle_scale = all_trains * number
    return (
        cycle_scale[:, None, None] * gram_rows / (means_rows[:, :, None] * means_whole[:, None, :])
    )


def solution(mesh):
    placed = (
        P("train", None, "pix"),
        P("train", None, "pix"),
        P(None, None, "pix"),
        P(None, "pix"),
        P("pix", None),
        P(),
    )
    return jax.shard_map(
        on_device, mesh=mesh, in_specs=placed, out_specs=P("pix", "train", None), check_vma=False
    )
```

profile of v0, /device:TPU:8, one launch (start us, length us, event | category | flops | bytes accessed | tf_op | source)
XLA Modules:
  0.0 208.9 jit_solution(14207055044721804327)
XLA Ops:
  6.5 0.0 copy-start.1
  6.5 0.0 copy-start
  6.5 0.0 copy-start.2
  6.5 0.0 all-reduce.2.cloned.1.call-start
  6.5 0.9 fusion.12
  7.4 0.8 copy.22
  8.2 0.2 fusion.7
  8.5 0.2 copy.23
  8.7 0.9 convert_reduce_fusion
  9.5 0.0 copy-done.1
  9.6 0.0 copy-done
  9.6 0.0 copy-done.2
  9.6 0.4 select_multiply_fusion
  10.0 0.4 copy.24
  10.4 1.9 scatter_custom_fusion
  12.2 1.1 reshape.82
  13.3 104.6 %all_to_all.24 = f32[64,3,2,1056]{3,2,1,0:T(2,128)S(1)} all-to-all(f32[64,3,2,1056]{3,2,1,0:T(2,128)S(1)} %reshape.82), channel_id=1, replica_groups=mesh['pix'=64,'train'=8] {'pix'}, dimensions={0} | all-to-all | bytes 3244032 | tf_op jit(solution)/shard_map/all_to_all | solution.py:38
  117.9 0.6 copy.25
  118.5 3.4 %reshape.83 = f32[3,128,3,352]{3,2,1,0:T(4,128)} reshape(f32[1,3,64,2,1056]{4,3,2,1,0:T(2,128)S(1)} %copy.25) | data formatting | bytes 3244032 | tf_op jit(solution)/shard_map/reshape | solution.py:41
  121.9 6.9 %fusion.2 = f32[3,352,352]{2,1,0:T(8,128)} fusion(f32[3,128,3,352]{3,2,1,0:T(4,128)} %reshape.83), kind=kOutput, calls=%fused_computation.3 | convolution fusion | flops 1712848896 | bytes 3108864 | tf_op jit(solution)/shard_map/kstf,kstg->kfg/dot_general | solution.py:42
  128.7 0.0 copy-start.3
  128.7 0.0 all-reduce.2.cloned.1.call-update
  128.8 0.7 copy-done.3
  129.4 0.1 select_reduce_fusion.1
  129.6 0.8 convert_element_type.29
  130.3 6.0 %all-to-all-start = ((f32[64,3,1]{1,2,0:T(1,128)}), f32[64,3,1]{1,2,0:T(1,128)S(1)}, u32[]{:S(2)}, u32[]{:S(2)}) async-start(f32[64,3,1]{1,2,0:T(1,128)} %bitcast.1), calls=%async_computation | async-start | bytes 65536 | tf_op jit(solution)/shard_map/all_to_all | solution.py:39
  136.3 13.7 %all-to-all-done = f32[64,3,1]{1,2,0:T(1,128)S(1)} async-done(((f32[64,3,1]{1,2,0:T(1,128)}), f32[64,3,1]{1,2,0:T(1,128)S(1)}, u32[]{:S(2)}, u32[]{:S(2)}) %all-to-all-start) | async-done | bytes 800 | tf_op jit(solution)/shard_map/all_to_all | solution.py:39
  150.0 0.1 reduce_sum.63
  150.1 0.4 bitcast_reduce_fusion
  150.5 0.1 reduce_sum.67
  150.6 12.8 %psum.15 = f32[3,352]{1,0:T(4,128)S(1)} all-reduce(f32[3,352]{1,0:T(4,128)S(1)} %reduce_sum.68), channel_id=1, replica_groups=mesh['pix'=64,'train'=8] {'train'}, use_global_device_ids=true, to_apply=%region_11.12 | all-reduce | flops 1056 | bytes 8448 | tf_op jit(solution)/shard_map/psum | solution.py:53
  163.5 0.1 constant_dynamic-slice_fusion
  163.5 36.8 %all-reduce.2.cloned.1.call-done = f32[3,352,352]{2,1,0:T(8,128)} async-done(((f32[3,352,352]{2,1,0:T(8,128)}), f32[3,352,352]{2,1,0:T(8,128)}) %all-reduce.2.cloned.1.call-update) | async-done | bytes 1486864 | tf_op jit(solution)/shard_map/psum | solution.py:53
  200.3 1.7 multiply_divide_fusion
  (11 shorter events, 0.2 us)
Async XLA Ops:
  6.5 3.0 %copy-start.1 = (bf16[3,352,256]{2,1,0:T(8,128)(2,1)S(1)}, bf16[3,352,256]{2,1,0:T(8,128)(2,1)}, u32[]{:S(2)}) copy-start(bf16[3,352,256]{2,1,0:T(8,128)(2,1)} %param.8) | copy-start | bytes 1622020
  6.5 3.1 %copy-start = (s32[3,352,256]{2,1,0:T(8,128)S(1)}, s32[3,352,256]{2,1,0:T(8,128)}, u32[]{:S(2)}) copy-start(s32[3,352,256]{2,1,0:T(8,128)} %param.7) | copy-start | bytes 3244036
  6.5 3.1 %copy-start.2 = (bf16[3,352,256]{2,1,0:T(8,128)(2,1)S(1)}, bf16[3,352,256]{2,1,0:T(8,128)(2,1)}, u32[]{:S(2)}) copy-start(bf16[3,352,256]{2,1,0:T(8,128)(2,1)} %param.6) | copy-start | bytes 1622020
  6.5 193.8 %all-reduce.2.cloned.1.call-start = ((), (), s32[]{:S(2)}) async-start(), calls=%async_computation.2 | async-start | bytes 3244032 | tf_op jit(solution)/shard_map/psum | solution.py:53
  128.7 0.7 copy-start.3
  130.3 19.7 %all-to-all-start = ((f32[64,3,1]{1,2,0:T(1,128)}), f32[64,3,1]{1,2,0:T(1,128)S(1)}, u32[]{:S(2)}, u32[]{:S(2)}) async-start(f32[64,3,1]{1,2,0:T(1,128)} %bitcast.1), calls=%async_computation | async-start | bytes 65536 | tf_op jit(solution)/shard_map/all_to_all | solution.py:39
Sparse Core Ops, SparseCore 0:
  128.9 71.4 all-reduce.1
where the time goes:
time: 209 us
  blocking collectives  117 us (56%)
  waiting for transfers between devices  50.5 us (24%)
  between operations  13.5 us (6%)
  local copies, waits for them, and re-layouts  10.7 us (5%)
  matrix products  6.85 us (3%)
  starting transfers between devices  5.95 us (3%)
  other arithmetic  3.88 us (2%)
    all_to_all x1, blocking collectives, on_device(): lax.all_to_all(buffer, 'pix', split_axis=0, concat_axis=2, tiled=True)  105 us
    psum x1, waiting for transfers between devices, on_device(): gram_whole, means_whole = lax.psum((gram_sum, frame_means), 'train')  36.8 us
    all_to_all x1, waiting for transfers between devices, on_device(): lax.all_to_all(cycle_tally, 'pix', split_axis=0, concat_axis=2, tiled=True)  13.7 us
    psum x1, blocking collectives, on_device(): gram_whole, means_whole = lax.psum((gram_sum, frame_means), 'train')  12.8 us
    dot_general x1, matrix products, on_device(): jnp.einsum('kstf,kstg->kfg', blocks, blocks, precision=lax.Precision.HIGH...  6.85 us
    all_to_all x1, starting transfers between devices, on_device(): lax.all_to_all(cycle_tally, 'pix', split_axis=0, concat_axis=2, tiled=True)  5.95 us
  transfers between devices with their start and end apart: 2, of which 2 were waited for; matrix products, arithmetic and copies ran while one was open for 1% of the time, Pallas kernels for 0%

commit v1 on v0

--- a/solution.py
+++ b/solution.py
@@ -35,7 +35,9 @@
     )
     buffer = buffer.reshape(owners, CYCLE_DEV, slot_depth, trains * pulses)
     cycle_tally = slot_counts.astype(jnp.float32).reshape(owners, CYCLE_DEV, 1)
-    slot_data = lax.all_to_all(buffer, "pix", split_axis=0, concat_axis=2, tiled=True)
+    pieces = jnp.split(buffer, lax.axis_size("pix"), axis=0)
+    arrived = lax.all_to_all(jnp.stack(pieces), "pix", 0, 0)
+    slot_data = jnp.concatenate(arrived, axis=2)
     numbers = lax.all_to_all(cycle_tally, "pix", split_axis=0, concat_axis=2, tiled=True)
     item_count = slot_data.shape[1]
     blocks = slot_data.reshape(item_count, slot_data.shape[2], trains, pulses)

time: 209 us -> 226 us (1.081)
  local copies, waits for them, and re-layouts: 10.7 us -> 25.5 us
    another operation x3 -> x69, local copies, waits for them, and re-layouts: 0.16 us -> 17.2 us  [the longest x65 13.6 us: on_device(): arrived = lax.all_to_all(jnp.stack(pieces), 'pix', 0, 0)]
    reshape x2 -> x1, local copies, waits for them, and re-layouts: 4.46 us -> 0.61 us  [on_device(): slot_data = jnp.concatenate(arrived, axis=2)]
where the time goes in v1:
time: 226 us; the launch traced here: 225 us
  blocking collectives  117 us (52%)
  waiting for transfers between devices  51.1 us (23%)
  local copies, waits for them, and re-layouts  25.5 us (11%)
  between operations  14.1 us (6%)
  matrix products  6.86 us (3%)
  starting transfers between devices  5.96 us (3%)
  other arithmetic  3.88 us (2%)
    all_to_all x1, blocking collectives, on_device(): arrived = lax.all_to_all(jnp.stack(pieces), 'pix', 0, 0)  105 us
    psum x1, waiting for transfers between devices, on_device(): gram_whole, means_whole = lax.psum((gram_sum, frame_means), 'train')  37.4 us
    all_to_all x1, waiting for transfers between devices, on_device(): lax.all_to_all(cycle_tally, 'pix', split_axis=0, concat_axis=2, tiled=True)  13.7 us
    another operation x65, local copies, waits for them, and re-layouts, on_device(): arrived = lax.all_to_all(jnp.stack(pieces), 'pix', 0, 0)  13.6 us
    psum x1, blocking collectives, on_device(): gram_whole, means_whole = lax.psum((gram_sum, frame_means), 'train')  12.8 us
    dot_general x1, matrix products, on_device(): jnp.einsum('kstf,kstg->kfg', blocks, blocks, precision=lax.Precision.HIGH...  6.86 us
    all_to_all x1, starting transfers between devices, on_device(): lax.all_to_all(cycle_tally, 'pix', split_axis=0, concat_axis=2, tiled=True)  5.96 us
  transfers between devices with their start and end apart: 2, of which 2 were waited for; matrix products, arithmetic and copies ran while one was open for 1% of the time, Pallas kernels for 0%

profile of v1, /device:TPU:8, one launch (start us, length us, event | category | flops | bytes accessed | tf_op | source)
XLA Modules:
  0.0 224.9 jit_solution(13249980173099840045)
XLA Ops:
  6.5 0.0 all-reduce.2.cloned.1.call-start
  6.5 0.9 fusion.16
  7.4 0.8 copy.22
  8.2 0.2 fusion.7
  8.5 0.2 copy.23
  8.7 0.9 convert_reduce_fusion
  9.5 0.0 copy-done.1
  9.6 0.0 copy-done
  9.6 0.0 copy-done.2
  9.6 0.4 select_multiply_fusion
  10.0 0.4 copy.24
  10.4 1.9 scatter_custom_fusion
  12.2 0.7 fusion.15
  12.9 0.7 fusion.14
  13.7 0.7 fusion.13
  14.3 0.8 stack.201
  15.1 0.8 stack.200
  15.9 0.8 stack.199
  16.7 0.8 stack.198
  17.5 0.8 stack.197
  18.3 0.8 stack.196
  19.1 0.8 stack.195
  19.9 0.8 stack.220
  20.7 0.8 stack.219
  21.4 0.8 stack.218
  22.2 0.8 stack.217
  23.0 0.8 stack.216
  23.8 0.8 stack.215
  24.6 0.8 stack.214
  25.4 0.8 stack.213
  26.5 0.8 stack.239
  29.3 104.6 %all_to_all.14 = f32[64,1,3,2,1056]{4,3,2,1,0:T(2,128)S(1)} all-to-all(f32[64,1,3,2,1056]{4,3,2,1,0:T(2,128)S(1)} %constant_dynamic-update-slice_fusion), channel_id=1, replica_groups=mesh['pix'=64,'train'=8] {'pix'}, dimensions={0} | all-to-all | bytes 3244032 | tf_op jit(solution)/shard_map/all_to_all | solution.py:39
  133.9 0.6 copy.25
  134.5 3.4 %reshape_reshape.3 = f32[3,128,3,352]{3,2,1,0:T(4,128)} reshape(f32[1,3,64,2,1056]{4,3,2,1,0:T(2,128)S(1)} %copy.25) | data formatting | bytes 3244032 | tf_op jit(solution)/shard_map/reshape;reshape | solution.py:43
  137.9 6.9 %fusion.2 = f32[3,352,352]{2,1,0:T(8,128)} fusion(f32[3,128,3,352]{3,2,1,0:T(4,128)} %reshape_reshape.3), kind=kOutput, calls=%fused_computation.3 | convolution fusion | flops 1712848896 | bytes 3108864 | tf_op jit(solution)/shard_map/kstf,kstg->kfg/dot_general | solution.py:44
  144.8 0.0 all-reduce.2.cloned.1.call-update
  144.8 0.0 copy-done.3
  144.8 0.1 select_reduce_fusion.1
  144.9 0.8 convert_element_type.29
  145.7 6.0 %all-to-all-start = ((f32[64,3,1]{1,2,0:T(1,128)}), f32[64,3,1]{1,2,0:T(1,128)S(1)}, u32[]{:S(2)}, u32[]{:S(2)}) async-start(f32[64,3,1]{1,2,0:T(1,128)} %bitcast.1), calls=%async_computation | async-start | bytes 65536 | tf_op jit(solution)/shard_map/all_to_all | solution.py:41
  151.7 13.7 %all-to-all-done = f32[64,3,1]{1,2,0:T(1,128)S(1)} async-done(((f32[64,3,1]{1,2,0:T(1,128)}), f32[64,3,1]{1,2,0:T(1,128)S(1)}, u32[]{:S(2)}, u32[]{:S(2)}) %all-to-all-start) | async-done | bytes 800 | tf_op jit(solution)/shard_map/all_to_all | solution.py:41
  165.4 0.1 reduce_sum.63
  165.5 0.4 bitcast_reduce_fusion
  165.9 0.1 reduce_sum.67
  166.0 12.8 %psum.15 = f32[3,352]{1,0:T(4,128)S(1)} all-reduce(f32[3,352]{1,0:T(4,128)S(1)} %reduce_sum.68), channel_id=1, replica_groups=mesh['pix'=64,'train'=8] {'train'}, use_global_device_ids=true, to_apply=%region_11.12 | all-reduce | flops 1056 | bytes 8448 | tf_op jit(solution)/shard_map/psum | solution.py:55
  178.8 0.1 constant_dynamic-slice_fusion
  178.9 37.4 %all-reduce.2.cloned.1.call-done = f32[3,352,352]{2,1,0:T(8,128)} async-done(((f32[3,352,352]{2,1,0:T(8,128)}), f32[3,352,352]{2,1,0:T(8,128)}) %all-reduce.2.cloned.1.call-update) | async-done | bytes 1486864 | tf_op jit(solution)/shard_map/psum | solution.py:55
  216.3 1.7 multiply_divide_fusion
  (128 shorter events, 2.0 us)
Async XLA Ops:
  6.5 3.0 %copy-start.1 = (bf16[3,352,256]{2,1,0:T(8,128)(2,1)S(1)}, bf16[3,352,256]{2,1,0:T(8,128)(2,1)}, u32[]{:S(2)}) copy-start(bf16[3,352,256]{2,1,0:T(8,128)(2,1)} %param.8) | copy-start | bytes 1622020
  6.5 3.1 %copy-start = (s32[3,352,256]{2,1,0:T(8,128)S(1)}, s32[3,352,256]{2,1,0:T(8,128)}, u32[]{:S(2)}) copy-start(s32[3,352,256]{2,1,0:T(8,128)} %param.7) | copy-start | bytes 3244036
  6.5 3.1 %copy-start.2 = (bf16[3,352,256]{2,1,0:T(8,128)(2,1)S(1)}, bf16[3,352,256]{2,1,0:T(8,128)(2,1)}, u32[]{:S(2)}) copy-start(bf16[3,352,256]{2,1,0:T(8,128)(2,1)} %param.6) | copy-start | bytes 1622020
  6.5 209.7 %all-reduce.2.cloned.1.call-start = ((), (), s32[]{:S(2)}) async-start(), calls=%async_computation.2 | async-start | bytes 3244032 | tf_op jit(solution)/shard_map/psum | solution.py:55
  137.9 6.9 %copy-start.3 = (s32[192]{0:T(256)S(1)}, s32[192]{0:T(256)}, u32[]{:S(2)}) copy-start(s32[192]{0:T(256)} %param.11) | copy-start | bytes 2308
  145.7 19.7 %all-to-all-start = ((f32[64,3,1]{1,2,0:T(1,128)}), f32[64,3,1]{1,2,0:T(1,128)S(1)}, u32[]{:S(2)}, u32[]{:S(2)}) async-start(f32[64,3,1]{1,2,0:T(1,128)} %bitcast.1), calls=%async_computation | async-start | bytes 65536 | tf_op jit(solution)/shard_map/all_to_all | solution.py:41
Sparse Core Ops, SparseCore 0:
  144.9 71.3 all-reduce.1
